TPU v7x, 256 devices: a whole 4x4x8 slice. The times are simulated.
256 devices in a mesh: clip: 16 (over z, core), row: 4 (over y), tm: 4 (over x).
Axes of the slice: x: 4, y: 4, z: 8, core: 2. Of those that a mesh axis runs over, the one named last changes fastest.
Arguments:
- frames: bfloat16 [128, 3, 16, 1024], P('clip', None, 'tm', 'row'), may hold values from -6 to 6
- keep_list: int32 [128], P('clip'), may hold values from -1 to 63, as said below
- train_slot: int32 [64], replicated, may hold values from 0 to 63, as said below
- stem_weight: bfloat16 [81, 128], replicated, may hold values from -0.625 to 0.625
- stem_gain: float32 [128], replicated, may hold values from 0.1 to 1.9
- stem_shift: float32 [128], replicated, may hold values from -3 to 3
- mixer_weight: bfloat16 [3, 3, 384, 256], replicated, may hold values from -0.109375 to 0.109375
- mixer_gain: float32 [256], replicated, may hold values from 0.1 to 1.9
- mixer_shift: float32 [256], replicated, may hold values from -3 to 3
- down_weight: bfloat16 [1024, 256], replicated, may hold values from -0.1875 to 0.1875
- down_bias: float32 [256], replicated, may hold values from -3 to 3
Outputs:
- latents: bfloat16 [64, 8, 8, 32, 256], P('clip', 'tm', 'row')
Inputs may be any that keep to these rules, and one draw needn't show every extreme that they name: `keep_list`: each encoder position 0 to 63 is named by exactly one slot, and -1 marks a dropped slot; encoder position e belongs to index e // 4 of clip. `train_slot`: A permutation; training position t belongs to index t // 4 of clip; at most 1 encoder positions of one index of clip go to one index of clip.
All inputs are finite; a program needn't handle non-finite values.
Results may differ from a plain program's by a relative error of at most 0.0053.
Values may be sent and summed in bfloat16 or wider, within the bound.
No kernel may reach another device: no remote copies, remote signals or barrier semaphores. Data moves between devices by JAX's collectives and lax.ppermute only.
A program may use at most 64 MiB of HBM per device.

v0:
```python
import jax
import jax.numpy as jnp
from jax import lax
from jax.sharding import PartitionSpec as P

GROUPS = 32
COLS = 64
eps = 1e-06


def from_behind(shard, axis, by):
    size = lax.axis_size(axis)
    pairs = [(i, i + by) for i in range(size) if 0 <= i + by < size]
    return lax.ppermute(shard, axis, pairs)


def extended_2(cells, sides, width):
    for axis, dim in sides:
        count = lax.axis_size(axis)
        ends = count - 1
        head = lax.slice_in_dim(cells, 0, width, axis=dim)
        tail = lax.slice_in_dim(cells, cells.shape[dim] - width, cells.shape[dim], axis=dim)
        cells = jnp.concatenate(
            [
                lax.ppermute(tail, axis, [(i, (i + 1) % count) for i in range(ends)]),
                cells,
                lax.ppermute(head, axis, [((i + 1) % count, i) for i in range(ends)]),
            ],
            axis=dim,
        )
    return cells


def surround_time(volume):
    frame_n = volume.shape[1]
    earlier = from_behind(volume[:, frame_n - 2 :], "tm", 1)
    opening = jnp.broadcast_to(volume[:, :1], earlier.shape)
    earlier = jnp.where(lax.axis_index("tm") == 0, opening, earlier)
    extended = jnp.concatenate([earlier, volume], axis=1)
    extended = extended_2(extended, (("row", 2),), 1)
    return jnp.pad(extended, ((0, 0), (0, 0), (0, 0), (1, 1), (0, 0)))


def norm_silu(hidden, gain, shift):
    batch_n, cell_n, chan_n = hidden.shape
    per_group = chan_n // GROUPS
    value_sum = jnp.sum(hidden, axis=1).reshape(batch_n, GROUPS, per_group).sum(-1)
    square_sum = jnp.sum(hidden * hidden, axis=1).reshape(batch_n, GROUPS, per_group).sum(-1)
    value_sum, square_sum = lax.psum((value_sum, square_sum), ("row", "tm"))
    cell_count = cell_n * per_group * lax.axis_size("row") * lax.axis_size("tm")
    group_mean = value_sum / cell_count
    spread = square_sum / cell_count - group_mean * group_mean
    inverse = lax.rsqrt(spread + eps)
    mean_full = jnp.repeat(group_mean, per_group, axis=1)[:, None, :]
    scale_full = jnp.repeat(inverse, per_group, axis=1)[:, None, :] * gain
    return jax.nn.silu((hidden - mean_full) * scale_full + shift)


def encode(clips, params, col_n, surround):
    (
        stem_weight,
        stem_gain,
        stem_shift,
        mixer_weight,
        mixer_gain,
        mixer_shift,
        down_weight,
        down_bias,
    ) = params
    batch_n, chan_in, frame_n, row_cells = clips.shape
    row_n = row_cells // col_n
    cell_n = frame_n * row_n * col_n
    volume = clips.reshape(batch_n, chan_in, frame_n, row_n, col_n).transpose(0, 2, 3, 4, 1)
    padded = surround(volume)
    tap_views = []
    for time_tap in range(3):
        for row_tap in range(3):
            for col_tap in range(3):
                tap_views.append(
                    padded[
                        :,
                        time_tap : time_tap + frame_n,
                        row_tap : row_tap + row_n,
                        col_tap : col_tap + col_n,
                    ]
                )
    patches = jnp.concatenate(tap_views, axis=-1).reshape(batch_n * cell_n, 27 * chan_in)
    stem = jnp.dot(patches, stem_weight, preferred_element_type=jnp.float32).reshape(
        batch_n, cell_n, -1
    )
    hidden = norm_silu(stem, stem_gain, stem_shift).astype(jnp.bfloat16)
    padded = surround(hidden.reshape(batch_n, frame_n, row_n, col_n, -1))
    accumulated = jnp.zeros((batch_n * cell_n, mixer_weight.shape[3]), jnp.float32)
    for time_tap in range(3):
        for row_tap in range(3):
            tap_strip = jnp.concatenate(
                [
                    padded[
                        :,
                        time_tap : time_tap + frame_n,
                        row_tap : row_tap + row_n,
                        col_tap : col_tap + col_n,
                    ]
                    for col_tap in range(3)
                ],
                axis=-1,
            )
            accumulated = accumulated + jnp.dot(
                tap_strip.reshape(-1, tap_strip.shape[-1]),
                mixer_weight[time_tap, row_tap],
                preferred_element_type=jnp.float32,
            )
    activated = norm_silu(accumulated.reshape(batch_n, cell_n, -1), mixer_gain, mixer_shift).astype(
        jnp.bfloat16
    )
    activated = activated.reshape(batch_n, frame_n, row_n, col_n, -1)
    pooled = (
        (activated[:, 0::2].astype(jnp.float32) + activated[:, 1::2].astype(jnp.float32)) * 0.5
    ).astype(jnp.bfloat16)
    chan_out = pooled.shape[-1]
    blocks = (
        pooled.reshape(batch_n, frame_n // 2, row_n // 2, 2, col_n // 2, 2, chan_out)
        .transpose(0, 1, 2, 4, 3, 5, 6)
        .reshape(-1, 4 * chan_out)
    )
    latent = jnp.dot(blocks, down_weight, preferred_element_type=jnp.float32) + down_bias
    return latent.astype(jnp.bfloat16).reshape(
        batch_n, frame_n // 2, row_n // 2, col_n // 2, chan_out
    )


def encode_layout(clips, params):
    return encode(clips, params, COLS, surround_time)


def select_rows(target, items, slot_n):
    flattened = items.reshape(items.shape[0], -1)
    wanted = jnp.arange(slot_n, dtype=jnp.int32)
    picker = (wanted[:, None] == target[None, :]).astype(jnp.bfloat16)
    return jnp.dot(picker, flattened, preferred_element_type=jnp.float32).astype(jnp.bfloat16)


def combine_sources(received):
    return jnp.sum(received.astype(jnp.float32), axis=0).astype(jnp.bfloat16)


def local(
    frames,
    keep_list,
    train_slot,
    stem_weight,
    stem_gain,
    stem_shift,
    mixer_weight,
    mixer_gain,
    mixer_shift,
    down_weight,
    down_bias,
):
    params = (
        stem_weight,
        stem_gain,
        stem_shift,
        mixer_weight,
        mixer_gain,
        mixer_shift,
        down_weight,
        down_bias,
    )
    group_n = lax.axis_size("clip")
    enc_dev = train_slot.shape[0] // group_n
    slot_n = group_n * enc_dev
    safe_keep = jnp.maximum(keep_list, 0)
    composed = jnp.where(keep_list >= 0, train_slot[safe_keep], -1)
    packed = select_rows(composed, frames, slot_n).reshape((group_n, enc_dev) + frames.shape[1:])
    received = lax.all_to_all(packed, "clip", split_axis=0, concat_axis=0, tiled=True)
    return encode_layout(combine_sources(received), params)


def solution(mesh):
    return jax.shard_map(
        local,
        mesh=mesh,
        in_specs=(
            P("clip", None, "tm", "row"),
            P("clip"),
            P(),
            P(),
            P(),
            P(),
            P(),
            P(),
            P(),
            P(),
            P(),
        ),
        out_specs=P("clip", "tm", "row", None, None),
        check_vma=False,
    )
```

profile of v0, /device:TPU:32, one launch (start us, length us, event | category | flops | bytes accessed | tf_op | source)
XLA Modules:
  0.0 240.4 jit_solution(16834706322915642902)
XLA Ops:
  1.6 1.3 gather_fusion
  4.8 8.6 %all-to-all-start = ((bf16[16,4,3,4,256]{4,3,2,1,0:T(4,128)(2,1)}), bf16[16,4,3,4,256]{4,3,2,1,0:T(4,128)(2,1)S(1)}, u32[]{:S(2)}, u32[]{:S(2)}) async-start(bf16[16,4,3,4,256]{4,3,2,1,0:T(4,128)(2,1)} %reshape.120), calls=%async_computation | async-start | bytes 786432 | tf_op jit(solution)/shard_map/all_to_all | solution.py:176
  13.4 11.9 %all-to-all-done = bf16[16,4,3,4,256]{4,3,2,1,0:T(4,128)(2,1)S(1)} async-done(((bf16[16,4,3,4,256]{4,3,2,1,0:T(4,128)(2,1)}), bf16[16,4,3,4,256]{4,3,2,1,0:T(4,128)(2,1)S(1)}, u32[]{:S(2)}, u32[]{:S(2)}) %all-to-all-start) | async-done | bytes 393248 | tf_op jit(solution)/shard_map/all_to_all | solution.py:176
  25.6 3.4 %collective-permute-start = (bf16[4,2,4,64,3]{3,2,4,1,0:T(4,128)(2,1)S(1)}, bf16[4,2,4,64,3]{3,2,4,1,0:T(4,128)(2,1)S(1)}, u32[]{:S(2)}, u32[]{:S(2)}) collective-permute-start(bf16[4,2,4,64,3]{3,2,4,1,0:T(4,128)(2,1)S(1)} %slice.325), channel_id=1, source_target_pairs={{0,1},{1,2},{2,3},{4,5},{5,6},{6,7},{8,9},{9,10},{10,11},{12,13},{... | collective-permute-start | bytes 36872 | tf_op jit(solution)/shard_map/ppermute | solution.py:14
  29.0 1.5 collective-permute-done
  32.0 4.5 %collective-permute-start.1 = (bf16[4,6,1,64,3]{3,2,4,1,0:T(2,128)(2,1)S(1)}, bf16[4,6,1,64,3]{3,2,4,1,0:T(2,128)(2,1)S(1)}, u32[]{:S(2)}, u32[]{:S(2)}) collective-permute-start(bf16[4,6,1,64,3]{3,2,4,1,0:T(2,128)(2,1)S(1)} %get-tuple-element.43), channel_id=1, source_target_pairs={{0,4},{4,8},{8,12},{1,5},{5,9},{9,13},{2,6},{6,10},{10,14},{3,7},{... | collective-permute-start | bytes 27656 | tf_op jit(solution)/shard_map/ppermute | solution.py:25
  36.5 1.6 collective-permute-done.1
  40.5 2.1 copy.36
  42.7 1.7 fusion.49
  44.7 42.5 %all-reduce.3 = (f32[4,32]{1,0:T(4,128)S(1)}, f32[4,32]{1,0:T(4,128)S(1)}) all-reduce(f32[4,32]{1,0:T(4,128)S(1)} %reduce_sum.88, f32[4,32]{1,0:T(4,128)S(1)} %reduce_sum.86), channel_id=1, replica_groups=mesh['clip'=16,'row'=4,'tm'=4] {'row','tm'}, use_global_device_ids=true, to_apply=%region_6.7 | all-reduce | flops 256 | bytes 2048 | tf_op jit(solution)/shard_map/psum | solution.py:49
  88.4 1.3 collective-permute-start.3
  89.7 6.6 %collective-permute-done.3 = bf16[4,2,4,64,128]{4,3,2,1,0:T(8,128)(2,1)S(1)} collective-permute-done((bf16[4,2,4,64,128]{4,3,2,1,0:T(8,128)(2,1)S(1)}, bf16[4,2,4,64,128]{4,3,2,1,0:T(8,128)(2,1)S(1)}, u32[]{:S(2)}, u32[]{:S(2)}) %collective-permute-start.3) | collective-permute-done | bytes 524320 | tf_op jit(solution)/shard_map/ppermute | solution.py:14
  97.8 4.8 %collective-permute-start.4 = (bf16[4,6,1,64,128]{4,3,2,1,0:T(8,128)(2,1)S(1)}, bf16[4,6,1,64,128]{4,3,2,1,0:T(8,128)(2,1)S(1)}, u32[]{:S(2)}, u32[]{:S(2)}) collective-permute-start(bf16[4,6,1,64,128]{4,3,2,1,0:T(8,128)(2,1)S(1)} %get-tuple-element.39), channel_id=1, source_target_pairs={{0,4},{4,8},{8,12},{1,5},{5,9},{9,13},{2,6},{6,10},{10,14},{3,7},{... | collective-permute-start | bytes 1179656 | tf_op jit(solution)/shard_map/ppermute | solution.py:25
  103.6 2.6 %collective-permute-done.5 = bf16[4,6,1,64,128]{4,3,2,1,0:T(8,128)(2,1)S(1)} collective-permute-done((bf16[4,6,1,64,128]{4,3,2,1,0:T(8,128)(2,1)S(1)}, bf16[4,6,1,64,128]{4,3,2,1,0:T(8,128)(2,1)S(1)}, u32[]{:S(2)}, u32[]{:S(2)}) %collective-permute-start.5) | collective-permute-done | bytes 393248 | tf_op jit(solution)/shard_map/ppermute | solution.py:27
  106.2 1.5 collective-permute-done.4
  107.6 1.4 select_maximum_fusion
  109.1 6.2 %fusion.50 = (bf16[4,4,4,64,128]{4,3,2,1,0:T(8,128)(2,1)}, bf16[4,4,4,64,128]{4,3,2,1,0:T(8,128)(2,1)}, bf16[4,4,4,64,128]{4,3,2,1,0:T(8,128)(2,1)}, bf16[4,4,4,...) fusion(bf16[4,6,6,66,128]{4,3,2,1,0:T(8,128)(2,1)S(1)} %select_, ...), kind=kLoop, calls=%fused_computation.143 | loop fusion | bytes 37748736 | tf_op jit(solution)/shard_map/slice | solution.py:98
  128.2 1.3 pad_maximum_fusion.5
  135.2 3.2 %bitcast_reduce_fusion = (f32[4,256]{1,0:T(4,128)S(1)}, f32[4,256]{1,0:T(4,128)S(1)}, f32[4096,256]{1,0:T(8,128)}) fusion(f32[4096,256]{1,0:T(8,128)S(1)} %convolution_add_fusion.1, bf16[4096,384]{1,0:T(8,128)(2,1)S(1)} %bitcast.87, bf16[3,3,384,256]{3,2,1,0:T(8,128)(2,1)S(1)} %copy-done.8), kind=kOutput, calls=%fused_computation.14 | convolution fusion | flops 809498624 | bytes 11739136 | tf_op jit(solution)/shard_map/dot_general | solution.py:108
  138.8 38.2 %all-reduce.2 = (f32[4,32]{1,0:T(4,128)S(1)}, f32[4,32]{1,0:T(4,128)S(1)}) all-reduce(f32[4,32]{1,0:T(4,128)S(1)} %reduce_sum.92, f32[4,32]{1,0:T(4,128)S(1)} %reduce_sum.90), channel_id=1, replica_groups=mesh['clip'=16,'row'=4,'tm'=4] {'row','tm'}, use_global_device_ids=true, to_apply=%region_12.13 | all-reduce | flops 256 | bytes 2048 | tf_op jit(solution)/shard_map/psum | solution.py:49
  177.4 6.2 %fusion.4 = bf16[4,4,4,64,256]{4,1,3,2,0:T(4,128)(2,1)S(1)} fusion(f32[4,4,4,64,256]{4,3,2,1,0:T(8,128)} %bitcast.86, f32[256]{0:T(256)S(1)} %copy-done.13, f32[4,256]{1,0:T(4,128)S(1)} %broadcast_multiply_fusion, f32[4,256]{1,0:T(4,128)S(1)} %sub.31), kind=kLoop, calls=%fused_computation.19 | loop fusion | flops 8388608 | bytes 6300672 | tf_op jit(solution)/shard_map/convert_element_type | solution.py:113
  183.6 25.5 %slice.321 = bf16[4,2,4,64,256]{4,1,3,2,0:T(2,128)(2,1)} slice(bf16[4,4,4,64,256]{4,1,3,2,0:T(4,128)(2,1)S(1)} %fusion.4), slice={[0:4:1], [1:4:2], [0:4:1], [0:64:1], [0:256:1]} | slice | bytes 2097152 | tf_op jit(solution)/shard_map/slice | solution.py:118
  209.1 25.4 %slice.320 = bf16[4,2,4,64,256]{4,1,3,2,0:T(2,128)(2,1)} slice(bf16[4,4,4,64,256]{4,1,3,2,0:T(4,128)(2,1)S(1)} %fusion.4), slice={[0:4:1], [0:4:2], [0:4:1], [0:64:1], [0:256:1]} | slice | bytes 2097152 | tf_op jit(solution)/shard_map/slice | solution.py:118
  234.5 3.1 %multiply_convert_fusion = bf16[4,2,4,64,256]{4,1,3,2,0:T(2,128)(2,1)S(1)} fusion(bf16[4,2,4,64,256]{4,1,3,2,0:T(2,128)(2,1)} %slice.321, bf16[4,2,4,64,256]{4,1,3,2,0:T(2,128)(2,1)} %slice.320), kind=kLoop, calls=%fused_computation.44 | loop fusion | flops 2621440 | bytes 3145728 | tf_op jit(solution)/shard_map/convert_element_type | solution.py:119
  (123 shorter events, 33.3 us)
Async XLA Ops:
  0.0 239.3 %copy-start = (bf16[1024,256]{1,0:T(8,128)(2,1)S(1)}, bf16[1024,256]{1,0:T(8,128)(2,1)}, u32[]{:S(2)}) copy-start(bf16[1024,256]{1,0:T(8,128)(2,1)} %param.20) | copy-start | bytes 1572868
  4.8 20.5 %all-to-all-start = ((bf16[16,4,3,4,256]{4,3,2,1,0:T(4,128)(2,1)}), bf16[16,4,3,4,256]{4,3,2,1,0:T(4,128)(2,1)S(1)}, u32[]{:S(2)}, u32[]{:S(2)}) async-start(bf16[16,4,3,4,256]{4,3,2,1,0:T(4,128)(2,1)} %reshape.120), calls=%async_computation | async-start | bytes 786432 | tf_op jit(solution)/shard_map/all_to_all | solution.py:176
  25.5 17.2 %copy-start.11 = (bf16[81,128]{1,0:T(8,128)(2,1)S(1)}, bf16[81,128]{1,0:T(8,128)(2,1)}, u32[]{:S(2)}) copy-start(bf16[81,128]{1,0:T(8,128)(2,1)} %param.14) | copy-start | bytes 62212
  25.6 4.9 %collective-permute-start = (bf16[4,2,4,64,3]{3,2,4,1,0:T(4,128)(2,1)S(1)}, bf16[4,2,4,64,3]{3,2,4,1,0:T(4,128)(2,1)S(1)}, u32[]{:S(2)}, u32[]{:S(2)}) collective-permute-start(bf16[4,2,4,64,3]{3,2,4,1,0:T(4,128)(2,1)S(1)} %slice.325), channel_id=1, source_target_pairs={{0,1},{1,2},{2,3},{4,5},{5,6},{6,7},{8,9},{9,10},{10,11},{12,13},{... | collective-permute-start | bytes 36872 | tf_op jit(solution)/shard_map/ppermute | solution.py:14
  30.7 5.9 %collective-permute-start.2 = (bf16[4,6,1,64,3]{3,2,4,1,0:T(2,128)(2,1)S(1)}, bf16[4,6,1,64,3]{3,2,4,1,0:T(2,128)(2,1)S(1)}, u32[]{:S(2)}, u32[]{:S(2)}) collective-permute-start(bf16[4,6,1,64,3]{3,2,4,1,0:T(2,128)(2,1)S(1)} %get-tuple-element.44), channel_id=1, source_target_pairs={{4,0},{8,4},{12,8},{5,1},{9,5},{13,9},{6,2},{10,6},{14,10},{7,3},{... | collective-permute-start | bytes 27656 | tf_op jit(solution)/shard_map/ppermute | solution.py:27
  32.0 6.2 %collective-permute-start.1 = (bf16[4,6,1,64,3]{3,2,4,1,0:T(2,128)(2,1)S(1)}, bf16[4,6,1,64,3]{3,2,4,1,0:T(2,128)(2,1)S(1)}, u32[]{:S(2)}, u32[]{:S(2)}) collective-permute-start(bf16[4,6,1,64,3]{3,2,4,1,0:T(2,128)(2,1)S(1)} %get-tuple-element.43), channel_id=1, source_target_pairs={{0,4},{4,8},{8,12},{1,5},{5,9},{9,13},{2,6},{6,10},{10,14},{3,7},{... | collective-permute-start | bytes 27656 | tf_op jit(solution)/shard_map/ppermute | solution.py:25
  40.3 47.4 %copy-start.14 = (f32[128]{0:T(128)S(1)}, f32[128]{0:T(128)}, u32[]{:S(2)}) copy-start(f32[128]{0:T(128)} %param.15) | copy-start | bytes 1540
  40.3 47.4 %copy-start.15 = (f32[128]{0:T(128)S(1)}, f32[128]{0:T(128)}, u32[]{:S(2)}) copy-start(f32[128]{0:T(128)} %param.16) | copy-start | bytes 1540
  88.4 8.0 %collective-permute-start.3 = (bf16[4,2,4,64,128]{4,3,2,1,0:T(8,128)(2,1)S(1)}, bf16[4,2,4,64,128]{4,3,2,1,0:T(8,128)(2,1)S(1)}, u32[]{:S(2)}, u32[]{:S(2)}) collective-permute-start(bf16[4,2,4,64,128]{4,3,2,1,0:T(8,128)(2,1)S(1)} %slice.357), channel_id=1, source_target_pairs={{0,1},{1,2},{2,3},{4,5},{5,6},{6,7},{8,9},{9,10},{10,11},{12,13},{... | collective-permute-start | bytes 1572872 | tf_op jit(solution)/shard_map/ppermute | solution.py:14
  96.5 9.7 %collective-permute-start.5 = (bf16[4,6,1,64,128]{4,3,2,1,0:T(8,128)(2,1)S(1)}, bf16[4,6,1,64,128]{4,3,2,1,0:T(8,128)(2,1)S(1)}, u32[]{:S(2)}, u32[]{:S(2)}) collective-permute-start(bf16[4,6,1,64,128]{4,3,2,1,0:T(8,128)(2,1)S(1)} %get-tuple-element.40), channel_id=1, source_target_pairs={{4,0},{8,4},{12,8},{5,1},{9,5},{13,9},{6,2},{10,6},{14,10},{7,3},{... | collective-permute-start | bytes 1179656 | tf_op jit(solution)/shard_map/ppermute | solution.py:27
  97.8 9.8 %collective-permute-start.4 = (bf16[4,6,1,64,128]{4,3,2,1,0:T(8,128)(2,1)S(1)}, bf16[4,6,1,64,128]{4,3,2,1,0:T(8,128)(2,1)S(1)}, u32[]{:S(2)}, u32[]{:S(2)}) collective-permute-start(bf16[4,6,1,64,128]{4,3,2,1,0:T(8,128)(2,1)S(1)} %get-tuple-element.39), channel_id=1, source_target_pairs={{0,4},{4,8},{8,12},{1,5},{5,9},{9,13},{2,6},{6,10},{10,14},{3,7},{... | collective-permute-start | bytes 1179656 | tf_op jit(solution)/shard_map/ppermute | solution.py:25
  116.7 1.2 copy-start.1
  116.7 1.5 copy-start.2
  116.7 1.8 copy-start.3
  118.6 1.5 copy-start.8
  124.9 1.3 copy-start.6
  124.9 1.5 copy-start.7
  130.8 1.3 copy-start.4
  130.8 1.5 copy-start.5
  132.4 1.2 copy-start.9
  132.4 1.5 copy-start.10
  135.2 42.1 %copy-start.12 = (f32[256]{0:T(256)S(1)}, f32[256]{0:T(256)}, u32[]{:S(2)}) copy-start(f32[256]{0:T(256)} %param.18) | copy-start | bytes 3076
  135.2 42.2 %copy-start.13 = (f32[256]{0:T(256)S(1)}, f32[256]{0:T(256)}, u32[]{:S(2)}) copy-start(f32[256]{0:T(256)} %param.19) | copy-start | bytes 3076
  234.5 4.8 %copy-start.16 = (f32[256]{0:T(256)S(1)}, f32[256]{0:T(256)}, u32[]{:S(2)}) copy-start(f32[256]{0:T(256)} %param.21) | copy-start | bytes 3076
where the time goes:
time: 241 us; the launch traced here: 240 us
  blocking collectives  80.7 us (33%)
  local copies, waits for them, and re-layouts  71.9 us (30%)
  waiting for transfers between devices  25.7 us (11%)
  starting transfers between devices  25.2 us (10%)
  other arithmetic  20.1 us (8%)
  matrix products  16.2 us (7%)
    psum x2, blocking collectives, norm_silu(): value_sum, square_sum = lax.psum((value_sum, square_sum), ('row', 'tm'))  80.7 us
    slice x1, local copies, waits for them, and re-layouts, encode(): activated[:, 1::2].astype(jnp.float32)  25.5 us
    slice x1, local copies, waits for them, and re-layouts, encode(): activated[:, 0::2].astype(jnp.float32)  25.4 us
    dot_general x9, matrix products, encode(): jnp.dot(tap_strip.reshape(-1, tap_strip.shape[-1]), mixer_weight[time_tap...  13.2 us
    all_to_all x1, waiting for transfers between devices, local(): lax.all_to_all(packed, 'clip', split_axis=0, concat_axis=0, tiled=True)  11.9 us
    ppermute x2, starting transfers between devices, extended_2(): lax.ppermute(tail, axis, [(i, (i + 1) % count) for i in range(ends)])  9.3 us
    all_to_all x1, starting transfers between devices, local(): lax.all_to_all(packed, 'clip', split_axis=0, concat_axis=0, tiled=True)  8.59 us
    slice x3, local copies, waits for them, and re-layouts, encode(): padded[:, time_tap:time_tap + frame_n, row_tap:row_tap + row_n, col_tap:c...  8.15 us
  transfers between devices with their start and end apart: 7, of which 6 were waited for; matrix products, arithmetic and copies ran while one was open for 0% of the time, Pallas kernels for 0%

commit v1 on v0

--- a/solution.py
+++ b/solution.py
@@ -46,7 +46,7 @@
     per_group = chan_n // GROUPS
     value_sum = jnp.sum(hidden, axis=1).reshape(batch_n, GROUPS, per_group).sum(-1)
     square_sum = jnp.sum(hidden * hidden, axis=1).reshape(batch_n, GROUPS, per_group).sum(-1)
-    value_sum, square_sum = lax.psum((value_sum, square_sum), ("row", "tm"))
+    value_sum, square_sum = lax.psum(lax.psum((value_sum, square_sum), "row"), "tm")
     cell_count = cell_n * per_group * lax.axis_size("row") * lax.axis_size("tm")
     group_mean = value_sum / cell_count
     spread = square_sum / cell_count - group_mean * group_mean

time: 241 us -> 205 us (0.85)
  blocking collectives: 80.7 us -> 43.6 us
    psum x2 -> x4, blocking collectives: 80.7 us -> 43.6 us  [the longest x2 22 us: norm_silu(): lax.psum((value_sum, square_sum), 'row')]
  transfers between devices with their start and end apart: 7 -> 7, of which waited for: 6 -> 6; matrix products, arithmetic and copies ran while one was open for 0% -> 1% of each run, Pallas kernels for 0% -> 0%
where the time goes in v1:
time: 205 us; the launch traced here: 204 us
  local copies, waits for them, and re-layouts  71.9 us (35%)
  blocking collectives  43.6 us (21%)
  waiting for transfers between devices  25.7 us (13%)
  starting transfers between devices  25.5 us (12%)
  other arithmetic  20.1 us (10%)
  matrix products  16.2 us (8%)
    slice x1, local copies, waits for them, and re-layouts, encode(): activated[:, 1::2].astype(jnp.float32)  25.5 us
    slice x1, local copies, waits for them, and re-layouts, encode(): activated[:, 0::2].astype(jnp.float32)  25.3 us
    psum x2, blocking collectives, norm_silu(): lax.psum((value_sum, square_sum), 'row')  22 us
    psum x2, blocking collectives, norm_silu(): lax.psum(lax.psum((value_sum, square_sum), 'row'), 'tm')  21.6 us
    dot_general x9, matrix products, encode(): jnp.dot(tap_strip.reshape(-1, tap_strip.shape[-1]), mixer_weight[time_tap...  13.2 us
    all_to_all x1, waiting for transfers between devices, local(): lax.all_to_all(packed, 'clip', split_axis=0, concat_axis=0, tiled=True)  11.9 us
    ppermute x2, starting transfers between devices, extended_2(): lax.ppermute(tail, axis, [(i, (i + 1) % count) for i in range(ends)])  9.3 us
    all_to_all x1, starting transfers between devices, local(): lax.all_to_all(packed, 'clip', split_axis=0, concat_axis=0, tiled=True)  8.59 us
  transfers between devices with their start and end apart: 7, of which 6 were waited for; matrix products, arithmetic and copies ran while one was open for 1% of the time, Pallas kernels for 0%

profile of v1, /device:TPU:32, one launch (start us, length us, event | category | flops | bytes accessed | tf_op | source)
XLA Modules:
  0.0 203.6 jit_solution(15095358037338295853)
XLA Ops:
  4.8 8.6 %all-to-all-start = ((bf16[16,4,3,4,256]{4,3,2,1,0:T(4,128)(2,1)}), bf16[16,4,3,4,256]{4,3,2,1,0:T(4,128)(2,1)S(1)}, u32[]{:S(2)}, u32[]{:S(2)}) async-start(bf16[16,4,3,4,256]{4,3,2,1,0:T(4,128)(2,1)} %reshape.120), calls=%async_computation | async-start | bytes 786432 | tf_op jit(solution)/shard_map/all_to_all | solution.py:176
  13.4 11.9 %all-to-all-done = bf16[16,4,3,4,256]{4,3,2,1,0:T(4,128)(2,1)S(1)} async-done(((bf16[16,4,3,4,256]{4,3,2,1,0:T(4,128)(2,1)}), bf16[16,4,3,4,256]{4,3,2,1,0:T(4,128)(2,1)S(1)}, u32[]{:S(2)}, u32[]{:S(2)}) %all-to-all-start) | async-done | bytes 393248 | tf_op jit(solution)/shard_map/all_to_all | solution.py:176
  25.6 3.4 %collective-permute-start = (bf16[4,2,4,64,3]{3,2,4,1,0:T(4,128)(2,1)S(1)}, bf16[4,2,4,64,3]{3,2,4,1,0:T(4,128)(2,1)S(1)}, u32[]{:S(2)}, u32[]{:S(2)}) collective-permute-start(bf16[4,2,4,64,3]{3,2,4,1,0:T(4,128)(2,1)S(1)} %slice.325), channel_id=1, source_target_pairs={{0,1},{1,2},{2,3},{4,5},{5,6},{6,7},{8,9},{9,10},{10,11},{12,13},{... | collective-permute-start | bytes 36872 | tf_op jit(solution)/shard_map/ppermute | solution.py:14
  29.0 1.5 collective-permute-done
  32.0 4.5 %collective-permute-start.1 = (bf16[4,6,1,64,3]{3,2,4,1,0:T(2,128)(2,1)S(1)}, bf16[4,6,1,64,3]{3,2,4,1,0:T(2,128)(2,1)S(1)}, u32[]{:S(2)}, u32[]{:S(2)}) collective-permute-start(bf16[4,6,1,64,3]{3,2,4,1,0:T(2,128)(2,1)S(1)} %get-tuple-element.47), channel_id=1, source_target_pairs={{0,4},{4,8},{8,12},{1,5},{5,9},{9,13},{2,6},{6,10},{10,14},{3,7},{... | collective-permute-start | bytes 27656 | tf_op jit(solution)/shard_map/ppermute | solution.py:25
  36.5 1.6 collective-permute-done.1
  40.5 2.1 %copy.36 = bf16[4,4,4,64,81]{4,3,2,1,0:T(8,128)(2,1)} copy(bf16[4,4,4,64,81]{3,2,4,1,0:T(4,128)(2,1)S(1)} %constant_dynamic-update-slice_fusion) | data formatting | bytes 1327104 | tf_op jit(solution)/shard_map/concatenate | solution.py:87
  42.7 1.6 fusion.49
  44.7 11.8 %all-reduce.5 = (f32[4,32]{1,0:T(4,128)S(1)}, f32[4,32]{1,0:T(4,128)S(1)}) all-reduce(f32[4,32]{1,0:T(4,128)S(1)} %reduce_sum.88, f32[4,32]{1,0:T(4,128)S(1)} %reduce_sum.86), channel_id=1, replica_groups=mesh['clip'=16,'row'=4,'tm'=4] {'row'}, use_global_device_ids=true, to_apply=%region_7.8 | all-reduce | flops 256 | bytes 2048 | tf_op jit(solution)/shard_map/psum | solution.py:49
  56.5 11.3 %all-reduce.3 = (f32[4,32]{1,0:T(4,128)S(1)}, f32[4,32]{1,0:T(4,128)S(1)}) all-reduce(f32[4,32]{1,0:T(4,128)S(1)} %get-tuple-element.15, f32[4,32]{1,0:T(4,128)S(1)} %get-tuple-element.16), channel_id=1, replica_groups=mesh['clip'=16,'row'=4,'tm'=4] {'tm'}, use_global_device_ids=true, to_apply=%region_8.9 | all-reduce | flops 256 | bytes 2048 | tf_op jit(solution)/shard_map/psum | solution.py:49
  68.9 1.6 collective-permute-start.3
  70.6 6.6 %collective-permute-done.3 = bf16[4,2,4,64,128]{4,3,2,1,0:T(8,128)(2,1)S(1)} collective-permute-done((bf16[4,2,4,64,128]{4,3,2,1,0:T(8,128)(2,1)S(1)}, bf16[4,2,4,64,128]{4,3,2,1,0:T(8,128)(2,1)S(1)}, u32[]{:S(2)}, u32[]{:S(2)}) %collective-permute-start.3) | collective-permute-done | bytes 524320 | tf_op jit(solution)/shard_map/ppermute | solution.py:14
  78.6 4.8 %collective-permute-start.4 = (bf16[4,6,1,64,128]{4,3,2,1,0:T(8,128)(2,1)S(1)}, bf16[4,6,1,64,128]{4,3,2,1,0:T(8,128)(2,1)S(1)}, u32[]{:S(2)}, u32[]{:S(2)}) collective-permute-start(bf16[4,6,1,64,128]{4,3,2,1,0:T(8,128)(2,1)S(1)} %get-tuple-element.43), channel_id=1, source_target_pairs={{0,4},{4,8},{8,12},{1,5},{5,9},{9,13},{2,6},{6,10},{10,14},{3,7},{... | collective-permute-start | bytes 1179656 | tf_op jit(solution)/shard_map/ppermute | solution.py:25
  84.4 2.6 %collective-permute-done.5 = bf16[4,6,1,64,128]{4,3,2,1,0:T(8,128)(2,1)S(1)} collective-permute-done((bf16[4,6,1,64,128]{4,3,2,1,0:T(8,128)(2,1)S(1)}, bf16[4,6,1,64,128]{4,3,2,1,0:T(8,128)(2,1)S(1)}, u32[]{:S(2)}, u32[]{:S(2)}) %collective-permute-start.5) | collective-permute-done | bytes 393248 | tf_op jit(solution)/shard_map/ppermute | solution.py:27
  87.0 1.5 collective-permute-done.4
  88.4 1.4 select_maximum_fusion
  89.9 6.3 %fusion.50 = (bf16[4,4,4,64,128]{4,3,2,1,0:T(8,128)(2,1)}, bf16[4,4,4,64,128]{4,3,2,1,0:T(8,128)(2,1)}, bf16[4,4,4,64,128]{4,3,2,1,0:T(8,128)(2,1)}, bf16[4,4,4,...) fusion(bf16[4,6,6,66,128]{4,3,2,1,0:T(8,128)(2,1)S(1)} %select_, ...), kind=kLoop, calls=%fused_computation.143 | loop fusion | bytes 37748736 | tf_op jit(solution)/shard_map/slice | solution.py:98
  116.1 3.2 %bitcast_reduce_fusion = (f32[4,256]{1,0:T(4,128)S(1)}, f32[4,256]{1,0:T(4,128)S(1)}, f32[4096,256]{1,0:T(8,128)}) fusion(f32[4096,256]{1,0:T(8,128)S(1)} %convolution_add_fusion.1, bf16[4096,384]{1,0:T(8,128)(2,1)S(1)} %bitcast.87, bf16[3,3,384,256]{3,2,1,0:T(8,128)(2,1)S(1)} %copy-done.8), kind=kOutput, calls=%fused_computation.14 | convolution fusion | flops 809498624 | bytes 11739136 | tf_op jit(solution)/shard_map/dot_general | solution.py:108
  119.6 10.2 %all-reduce.4 = (f32[4,32]{1,0:T(4,128)S(1)}, f32[4,32]{1,0:T(4,128)S(1)}) all-reduce(f32[4,32]{1,0:T(4,128)S(1)} %reduce_sum.92, f32[4,32]{1,0:T(4,128)S(1)} %reduce_sum.90), channel_id=1, replica_groups=mesh['clip'=16,'row'=4,'tm'=4] {'row'}, use_global_device_ids=true, to_apply=%region_15.16 | all-reduce | flops 256 | bytes 2048 | tf_op jit(solution)/shard_map/psum | solution.py:49
  129.9 10.3 %all-reduce.2 = (f32[4,32]{1,0:T(4,128)S(1)}, f32[4,32]{1,0:T(4,128)S(1)}) all-reduce(f32[4,32]{1,0:T(4,128)S(1)} %get-tuple-element.13, f32[4,32]{1,0:T(4,128)S(1)} %get-tuple-element.14), channel_id=1, replica_groups=mesh['clip'=16,'row'=4,'tm'=4] {'tm'}, use_global_device_ids=true, to_apply=%region_16.17 | all-reduce | flops 256 | bytes 2048 | tf_op jit(solution)/shard_map/psum | solution.py:49
  140.6 6.2 %fusion.4 = bf16[4,4,4,64,256]{4,1,3,2,0:T(4,128)(2,1)S(1)} fusion(f32[4,4,4,64,256]{4,3,2,1,0:T(8,128)} %bitcast.86, f32[256]{0:T(256)S(1)} %copy-done.13, f32[4,256]{1,0:T(4,128)S(1)} %broadcast_multiply_fusion, f32[4,256]{1,0:T(4,128)S(1)} %sub.31), kind=kLoop, calls=%fused_computation.19 | loop fusion | flops 8388608 | bytes 6300672 | tf_op jit(solution)/shard_map/convert_element_type | solution.py:113
  146.8 25.5 %slice.321 = bf16[4,2,4,64,256]{4,1,3,2,0:T(2,128)(2,1)} slice(bf16[4,4,4,64,256]{4,1,3,2,0:T(4,128)(2,1)S(1)} %fusion.4), slice={[0:4:1], [1:4:2], [0:4:1], [0:64:1], [0:256:1]} | slice | bytes 2097152 | tf_op jit(solution)/shard_map/slice | solution.py:118
  172.3 25.3 %slice.320 = bf16[4,2,4,64,256]{4,1,3,2,0:T(2,128)(2,1)} slice(bf16[4,4,4,64,256]{4,1,3,2,0:T(4,128)(2,1)S(1)} %fusion.4), slice={[0:4:1], [0:4:2], [0:4:1], [0:64:1], [0:256:1]} | slice | bytes 2097152 | tf_op jit(solution)/shard_map/slice | solution.py:118
  197.6 3.1 %multiply_convert_fusion = bf16[4,2,4,64,256]{4,1,3,2,0:T(2,128)(2,1)S(1)} fusion(bf16[4,2,4,64,256]{4,1,3,2,0:T(2,128)(2,1)} %slice.321, bf16[4,2,4,64,256]{4,1,3,2,0:T(2,128)(2,1)} %slice.320), kind=kLoop, calls=%fused_computation.44 | loop fusion | flops 2621440 | bytes 3145728 | tf_op jit(solution)/shard_map/convert_element_type | solution.py:119
  (125 shorter events, 36.0 us)
Async XLA Ops:
  0.0 202.4 %copy-start = (bf16[1024,256]{1,0:T(8,128)(2,1)S(1)}, bf16[1024,256]{1,0:T(8,128)(2,1)}, u32[]{:S(2)}) copy-start(bf16[1024,256]{1,0:T(8,128)(2,1)} %param.20) | copy-start | bytes 1572868
  4.8 20.5 %all-to-all-start = ((bf16[16,4,3,4,256]{4,3,2,1,0:T(4,128)(2,1)}), bf16[16,4,3,4,256]{4,3,2,1,0:T(4,128)(2,1)S(1)}, u32[]{:S(2)}, u32[]{:S(2)}) async-start(bf16[16,4,3,4,256]{4,3,2,1,0:T(4,128)(2,1)} %reshape.120), calls=%async_computation | async-start | bytes 786432 | tf_op jit(solution)/shard_map/all_to_all | solution.py:176
  25.5 17.2 %copy-start.11 = (bf16[81,128]{1,0:T(8,128)(2,1)S(1)}, bf16[81,128]{1,0:T(8,128)(2,1)}, u32[]{:S(2)}) copy-start(bf16[81,128]{1,0:T(8,128)(2,1)} %param.14) | copy-start | bytes 62212
  25.6 4.9 %collective-permute-start = (bf16[4,2,4,64,3]{3,2,4,1,0:T(4,128)(2,1)S(1)}, bf16[4,2,4,64,3]{3,2,4,1,0:T(4,128)(2,1)S(1)}, u32[]{:S(2)}, u32[]{:S(2)}) collective-permute-start(bf16[4,2,4,64,3]{3,2,4,1,0:T(4,128)(2,1)S(1)} %slice.325), channel_id=1, source_target_pairs={{0,1},{1,2},{2,3},{4,5},{5,6},{6,7},{8,9},{9,10},{10,11},{12,13},{... | collective-permute-start | bytes 36872 | tf_op jit(solution)/shard_map/ppermute | solution.py:14
  30.7 5.9 %collective-permute-start.2 = (bf16[4,6,1,64,3]{3,2,4,1,0:T(2,128)(2,1)S(1)}, bf16[4,6,1,64,3]{3,2,4,1,0:T(2,128)(2,1)S(1)}, u32[]{:S(2)}, u32[]{:S(2)}) collective-permute-start(bf16[4,6,1,64,3]{3,2,4,1,0:T(2,128)(2,1)S(1)} %get-tuple-element.48), channel_id=1, source_target_pairs={{4,0},{8,4},{12,8},{5,1},{9,5},{13,9},{6,2},{10,6},{14,10},{7,3},{... | collective-permute-start | bytes 27656 | tf_op jit(solution)/shard_map/ppermute | solution.py:27
  32.0 6.2 %collective-permute-start.1 = (bf16[4,6,1,64,3]{3,2,4,1,0:T(2,128)(2,1)S(1)}, bf16[4,6,1,64,3]{3,2,4,1,0:T(2,128)(2,1)S(1)}, u32[]{:S(2)}, u32[]{:S(2)}) collective-permute-start(bf16[4,6,1,64,3]{3,2,4,1,0:T(2,128)(2,1)S(1)} %get-tuple-element.47), channel_id=1, source_target_pairs={{0,4},{4,8},{8,12},{1,5},{5,9},{9,13},{2,6},{6,10},{10,14},{3,7},{... | collective-permute-start | bytes 27656 | tf_op jit(solution)/shard_map/ppermute | solution.py:25
  40.3 27.9 %copy-start.14 = (f32[128]{0:T(128)S(1)}, f32[128]{0:T(128)}, u32[]{:S(2)}) copy-start(f32[128]{0:T(128)} %param.15) | copy-start | bytes 1540
  40.3 27.9 %copy-start.15 = (f32[128]{0:T(128)S(1)}, f32[128]{0:T(128)}, u32[]{:S(2)}) copy-start(f32[128]{0:T(128)} %param.16) | copy-start | bytes 1540
  68.9 8.2 %collective-permute-start.3 = (bf16[4,2,4,64,128]{4,3,2,1,0:T(8,128)(2,1)S(1)}, bf16[4,2,4,64,128]{4,3,2,1,0:T(8,128)(2,1)S(1)}, u32[]{:S(2)}, u32[]{:S(2)}) collective-permute-start(bf16[4,2,4,64,128]{4,3,2,1,0:T(8,128)(2,1)S(1)} %slice.357), channel_id=1, source_target_pairs={{0,1},{1,2},{2,3},{4,5},{5,6},{6,7},{8,9},{9,10},{10,11},{12,13},{... | collective-permute-start | bytes 1572872 | tf_op jit(solution)/shard_map/ppermute | solution.py:14
  77.3 9.7 %collective-permute-start.5 = (bf16[4,6,1,64,128]{4,3,2,1,0:T(8,128)(2,1)S(1)}, bf16[4,6,1,64,128]{4,3,2,1,0:T(8,128)(2,1)S(1)}, u32[]{:S(2)}, u32[]{:S(2)}) collective-permute-start(bf16[4,6,1,64,128]{4,3,2,1,0:T(8,128)(2,1)S(1)} %get-tuple-element.44), channel_id=1, source_target_pairs={{4,0},{8,4},{12,8},{5,1},{9,5},{13,9},{6,2},{10,6},{14,10},{7,3},{... | collective-permute-start | bytes 1179656 | tf_op jit(solution)/shard_map/ppermute | solution.py:27
  78.6 9.8 %collective-permute-start.4 = (bf16[4,6,1,64,128]{4,3,2,1,0:T(8,128)(2,1)S(1)}, bf16[4,6,1,64,128]{4,3,2,1,0:T(8,128)(2,1)S(1)}, u32[]{:S(2)}, u32[]{:S(2)}) collective-permute-start(bf16[4,6,1,64,128]{4,3,2,1,0:T(8,128)(2,1)S(1)} %get-tuple-element.43), channel_id=1, source_target_pairs={{0,4},{4,8},{8,12},{1,5},{5,9},{9,13},{2,6},{6,10},{10,14},{3,7},{... | collective-permute-start | bytes 1179656 | tf_op jit(solution)/shard_map/ppermute | solution.py:25
  97.6 1.2 copy-start.1
  97.6 1.5 copy-start.2
  97.6 1.8 copy-start.3
  99.4 1.5 copy-start.8
  105.7 1.3 copy-start.6
  105.8 1.5 copy-start.7
  111.7 1.3 copy-start.4
  111.7 1.5 copy-start.5
  113.2 1.2 copy-start.9
  113.2 1.5 copy-start.10
  116.0 24.5 %copy-start.12 = (f32[256]{0:T(256)S(1)}, f32[256]{0:T(256)}, u32[]{:S(2)}) copy-start(f32[256]{0:T(256)} %param.18) | copy-start | bytes 3076
  116.1 24.5 %copy-start.13 = (f32[256]{0:T(256)S(1)}, f32[256]{0:T(256)}, u32[]{:S(2)}) copy-start(f32[256]{0:T(256)} %param.19) | copy-start | bytes 3076
  197.6 4.8 %copy-start.16 = (f32[256]{0:T(256)S(1)}, f32[256]{0:T(256)}, u32[]{:S(2)}) copy-start(f32[256]{0:T(256)} %param.21) | copy-start | bytes 3076
